TPU v7x, 256 devices: a whole 4x4x8 slice. The times are simulated.
256 devices in a mesh: tm: 32 (over y, x, core), space: 8 (over z).
Axes of the slice: x: 4, y: 4, z: 8, core: 2. Of those that a mesh axis runs over, the one named last changes fastest.
Arguments:
- latent_tokens: bfloat16 [64, 1792, 2240], P('tm', 'space'), may hold values from -6 to 6
- norm_gain: float32 [2240], replicated, may hold values from 0.5 to 1.5
- w_query: bfloat16 [2240, 1120], P('tm', 'space'), may hold values from -0.125 to 0.125
- w_key: bfloat16 [2240, 1120], P('tm', 'space'), may hold values from -0.125 to 0.125
- w_value: bfloat16 [2240, 1120], P('tm', 'space'), may hold values from -0.125 to 0.125
- out_gain: float32 [1120], replicated, may hold values from 0.5 to 1.5
- block_ids: int32 [64], P('tm'), may hold values from 0 to 15, never falling along the last dimension, each value on 1 to 8 neighbouring positions
Outputs:
- attended: bfloat16 [64, 1792, 1120], P('tm', 'space')
Inputs may be any that keep to these rules, and one draw needn't show every extreme that they name: `block_ids`: block numbers never fall from one frame to the next; each of the 16 blocks holds 1 to 8 frames and one holds exactly 8.
All inputs are finite; a program needn't handle non-finite values.
Results may differ from a plain program's by a relative error of at most 0.0065.
Values may be sent and summed in bfloat16 or wider, within the bound.
A program may use at most 192 MiB of HBM per device.

v0:
```python
import jax
import jax.numpy as jnp
from jax import lax
from jax.sharding import PartitionSpec as P

HEAD = 112
HEADS = 10


def gathered(weights):
    columns_full = lax.all_gather(jnp.stack(weights), "space", axis=2, tiled=True)
    return lax.all_gather(columns_full, "tm", axis=1, tiled=True)


def on_device(latent_tokens, norm_gain, w_query, w_key, w_value, out_gain, block_ids):
    frame_count, token_count, width = latent_tokens.shape
    row_count = frame_count * token_count
    values = latent_tokens.reshape(row_count, width).astype(jnp.float32)
    meansq = jnp.mean(values * values, axis=-1, keepdims=True)
    normed = (values * lax.rsqrt(meansq + 1e-06) * norm_gain).astype(jnp.bfloat16)
    pair = gathered((w_key, w_value))
    alone = gathered((w_query,))
    projected = jnp.einsum("rn,cnh->crh", normed, pair, preferred_element_type=jnp.float32)
    channels = projected.shape[2]
    headed = (frame_count, token_count, HEADS, HEAD)
    key = jax.nn.relu(projected[0]).astype(jnp.bfloat16).reshape(headed)
    value = projected[1].astype(jnp.bfloat16).reshape(headed)
    states = jnp.einsum("fthk,fthv->fhkv", key, value, preferred_element_type=jnp.float32)
    states = states.reshape(frame_count, channels, HEAD)
    mine = lax.psum_scatter(states, "space", scatter_dimension=1, tiled=True)
    everyone = lax.all_gather(mine.astype(jnp.bfloat16), "tm", tiled=True)
    all_ids = lax.all_gather(block_ids, "tm", tiled=True)
    reaches = (all_ids[None, :] <= block_ids[:, None]).astype(jnp.bfloat16)
    carried = jnp.einsum("fg,gkv->fkv", reaches, everyone, preferred_element_type=jnp.float32)
    carried = lax.all_gather(carried.astype(jnp.bfloat16), "space", axis=1, tiled=True)
    carried = carried.reshape(frame_count, HEADS, HEAD, HEAD)
    query = jnp.einsum("rn,cnh->crh", normed, alone, preferred_element_type=jnp.float32)[0]
    query = jax.nn.relu(query).astype(jnp.bfloat16).reshape(headed)
    numerator = jnp.einsum("fthk,fhkv->fthv", query, carried, preferred_element_type=jnp.float32)
    head_meansq = jnp.mean(numerator * numerator, axis=-1, keepdims=True)
    result = numerator * lax.rsqrt(head_meansq + 1e-06) * out_gain.reshape(HEADS, HEAD)
    return result.reshape(frame_count, token_count, channels).astype(jnp.bfloat16)


def solution(mesh):
    placed = (
        P("tm", "space", None),
        P(),
        P("tm", "space"),
        P("tm", "space"),
        P("tm", "space"),
        P(),
        P("tm"),
    )
    return jax.shard_map(
        on_device, mesh=mesh, in_specs=placed, out_specs=P("tm", "space", None), check_vma=False
    )
```

profile of v0, /device:TPU:6, one launch (start us, length us, event | category | flops | bytes accessed | tf_op | source)
XLA Modules:
  0.0 274.6 jit_solution(4759564278663120340)
XLA Ops:
  6.5 0.9 pad_maximum_fusion
  7.5 0.1 copy.40
  7.6 29.2 %all_gather.22 = bf16[2,70,1120]{1,0,2:T(2,128)(2,1)S(1)} all-gather(bf16[2,70,140]{1,0,2:T(2,128)(2,1)S(1)} %copy.40), channel_id=1, replica_groups=mesh['tm'=32,'space'=8] {'space'}, dimensions={2}, use_global_device_ids=true | all-gather | bytes 352800 | tf_op jit(solution)/shard_map/all_gather | solution.py:11
  36.9 2.2 copy.41
  39.2 25.1 %all-gather.2 = bf16[8,140,70]{2,1,0:T(8,128)(2,1)S(1)} all-gather(bf16[1,140,70]{2,1,0:T(8,128)(2,1)S(1)} %bitcast.50), channel_id=2, replica_groups=mesh['tm'=32,'space'=8] {'space'}, dimensions={0}, use_global_device_ids=true | all-gather | bytes 176400 | tf_op jit(solution)/shard_map/all_gather | solution.py:11
  64.4 0.9 copy.65
  65.3 0.5 multiply_reduce_fusion
  65.9 0.6 dynamic-slice.1
  67.1 1.8 fusion.3
  68.9 32.0 %all-gather.8.cloned.1.call-done = bf16[2,2240,1120]{2,0,1:T(2,128)(2,1)} async-done(((bf16[2,70,1120]{2,0,1:T(2,128)(2,1)}), bf16[2,2240,1120]{2,0,1:T(2,128)(2,1)}) %all-gather.8.cloned.1.call-update) | async-done | bytes 10035216 | tf_op jit(solution)/shard_map/all_gather | solution.py:12
  100.9 9.5 %fusion.4 = bf16[2,448,1120]{2,1,0:T(8,128)(2,1)S(1)} fusion(bf16[2,2240,1120]{2,0,1:T(2,128)(2,1)} %all-gather.8.cloned.1.call-done, bf16[448,2240]{1,0:T(8,128)(2,1)} %fusion.3), kind=kOutput, calls=%fused_computation.7 | convolution fusion | flops 4495769600 | bytes 14049280 | tf_op jit(solution)/shard_map/rn,cnh->crh/dot_general | solution.py:23
  110.4 1.2 fusion.14
  111.6 4.4 %reshape.88 = bf16[2,224,10,112]{3,2,1,0:T(8,128)(2,1)} reshape(bf16[1,448,1120]{2,1,0:T(8,128)(2,1)} %get-tuple-element.5) | data formatting | bytes 2007040 | tf_op jit(solution)/shard_map/convert_element_type | solution.py:26
  116.0 3.1 %reshape.89 = bf16[2,224,10,112]{3,2,1,0:T(8,128)(2,1)} reshape(bf16[1,448,1120]{2,1,0:T(8,128)(2,1)S(1)} %get-tuple-element.6) | data formatting | bytes 2007040 | tf_op jit(solution)/shard_map/convert_element_type | solution.py:27
  119.1 2.6 fusion.18
  121.8 4.2 %copy.47 = f32[2,1120,112]{2,0,1:T(2,128)S(1)} copy(f32[2,1120,112]{2,1,0:T(8,128)S(1)} %bitcast.46) | data formatting | bytes 2007040 | tf_op jit(solution)/shard_map/reshape | solution.py:29
  126.0 62.4 %all-reduce.3 = bf16[2,1120,112]{2,0,1:T(2,128)(2,1)} all-reduce(f32[2,1120,112]{2,0,1:T(2,128)S(1)} %copy.47), channel_id=4, replica_groups=mesh['tm'=32,'space'=8] {'space'}, use_global_device_ids=true, to_apply=%region_1.2.clone | all-reduce | flops 250880 | bytes 1505280
  188.4 0.9 dynamic-slice_convert_fusion
  189.3 0.6 copy.48
  190.1 0.6 dynamic-slice
  191.3 0.2 dynamic-update-slice
  191.5 14.1 %all-reduce = s32[64]{0:T(128)S(1)} all-reduce(s32[64]{0:T(128)S(1)} %dynamic-update-slice), channel_id=1, replica_groups=mesh['tm'=32,'space'=8] {'tm'}, use_global_device_ids=true, to_apply=%add | all-reduce | flops 64 | bytes 512
  205.6 1.9 multiply_convert_fusion
  207.5 8.1 %reshape.83 = bf16[2240,1120]{1,0:T(8,128)(2,1)} reshape(bf16[32,70,1120]{2,1,0:T(8,128)(2,1)} %all-gather.12.cloned.1.call-done) | data formatting | bytes 10035200
  215.6 5.3 %fusion.8 = bf16[1,448,1120]{2,1,0:T(8,128)(2,1)S(1)} fusion(bf16[448,2240]{1,0:T(8,128)(2,1)S(1)} %bitcast.48, bf16[2240,1120]{1,0:T(8,128)(2,1)} %reshape.83), kind=kOutput, calls=%fused_computation.10 | convolution fusion | flops 2248888320 | bytes 8028160 | tf_op jit(solution)/shard_map/rn,cnh->crh/dot_general | solution.py:37
  220.9 2.2 reshape.91
  223.1 13.1 %all-gather.10.cloned.1.call-done = bf16[64,140,112]{2,1,0:T(8,128)(2,1)} async-done(((bf16[2,140,112]{2,1,0:T(8,128)(2,1)}), bf16[64,140,112]{2,1,0:T(8,128)(2,1)}) %all-gather.10.cloned.1.call-update) | async-done | bytes 2007056 | tf_op jit(solution)/shard_map/all_gather | solution.py:31
  236.2 2.2 fusion.21
  238.4 27.0 %all_gather.25 = bf16[2,1120,112]{2,0,1:T(2,128)(2,1)S(1)} all-gather(bf16[2,140,112]{2,0,1:T(2,128)(2,1)S(1)} %fusion.21), channel_id=1, replica_groups=mesh['tm'=32,'space'=8] {'space'}, dimensions={1}, use_global_device_ids=true | all-gather | bytes 564480 | tf_op jit(solution)/shard_map/all_gather | solution.py:35
  265.4 0.9 fusion.9
  266.3 0.4 fusion.11
  266.7 1.4 copy.56
  (30 shorter events, 0.6 us)
Async XLA Ops:
  6.5 32.6 %copy-start.3 = (bf16[70,140]{1,0:T(8,128)(2,1)S(1)}, bf16[70,140]{1,0:T(8,128)(2,1)}, u32[]{:S(2)}) copy-start(bf16[70,140]{1,0:T(8,128)(2,1)} %param.9) | copy-start | bytes 58804
  6.5 58.8 %copy-start = (bf16[2,224,2240]{2,1,0:T(8,128)(2,1)S(1)}, bf16[2,224,2240]{2,1,0:T(8,128)(2,1)}, u32[]{:S(2)}) copy-start(bf16[2,224,2240]{2,1,0:T(8,128)(2,1)} %param.7) | copy-start | bytes 6021124
  6.5 94.4 %all-gather.8.cloned.1.call-start = ((), (), s32[]{:S(2)}) async-start(), calls=%async_computation | async-start | bytes 10644480 | tf_op jit(solution)/shard_map/all_gather | solution.py:12
  39.0 26.9 %copy-start.7 = (u32[256]{0:T(256)S(1)}, u32[256]{0:T(256)}, u32[]{:S(2)}) copy-start(u32[256]{0:T(256)} %constant.27) | copy-start | bytes 3076
  39.0 28.0 %copy-start.2 = (f32[2240]{0:T(1024)S(1)}, f32[2240]{0:T(1024)}, u32[]{:S(2)}) copy-start(f32[2240]{0:T(1024)} %param.8) | copy-start | bytes 26884
  39.1 168.4 %all-gather.12.cloned.1.call-start = ((), (), s32[]{:S(2)}) async-start(), calls=%async_computation.2 | async-start | bytes 5474304 | tf_op jit(solution)/shard_map/all_gather | solution.py:12
  65.3 170.9 %all-gather.10.cloned.1.call-start = ((), (), s32[]{:S(2)}) async-start(), calls=%async_computation.1 | async-start | bytes 2433024 | tf_op jit(solution)/shard_map/all_gather | solution.py:31
  121.8 68.2 %copy-start.4 = (f32[1120]{0:T(1024)S(1)}, f32[1120]{0:T(1024)}, u32[]{:S(2)}) copy-start(f32[1120]{0:T(1024)} %param.12) | copy-start | bytes 13444
  121.8 68.3 %copy-start.6 = (u32[256]{0:T(256)S(1)}, u32[256]{0:T(256)}, u32[]{:S(2)}) copy-start(u32[256]{0:T(256)} %constant.21) | copy-start | bytes 3076
  121.8 69.4 %copy-start.5 = (s32[2]{0:T(128)S(1)}, s32[2]{0:T(128)}, u32[]{:S(2)}) copy-start(s32[2]{0:T(128)} %param.13) | copy-start | bytes 28
  207.5 8.1 %copy-start.1 = (bf16[2,224,2240]{2,1,0:T(8,128)(2,1)S(1)}, bf16[2,224,2240]{2,1,0:T(8,128)(2,1)}, u32[]{:S(2)}) copy-start(bf16[2,224,2240]{2,1,0:T(8,128)(2,1)} %multiply_convert_fusion) | copy-start | bytes 6021124
Sparse Core Ops, SparseCore 0:
  39.2 61.6 all-gather.7
  103.5 51.7 all-gather.11
  190.1 46.0 all-gather.9
where the time goes:
time: 275 us
  blocking collectives  158 us (57%)
  waiting for transfers between devices  45.1 us (16%)
  local copies, waits for them, and re-layouts  29.9 us (11%)
  matrix products  20.5 us (7%)
  between operations  14.4 us (5%)
  other arithmetic  6.73 us (2%)
    unnamed x2, blocking collectives  76.5 us
    all_gather x2, blocking collectives, gathered(): lax.all_gather(jnp.stack(weights), 'space', axis=2, tiled=True)  54.3 us
    all_gather x2, waiting for transfers between devices, gathered(): return lax.all_gather(columns_full, 'tm', axis=1, tiled=True)  32 us
    all_gather x1, blocking collectives, on_device(): lax.all_gather(carried.astype(jnp.bfloat16), 'space', axis=1, tiled=True)  27 us
    all_gather x1, waiting for transfers between devices, on_device(): everyone = lax.all_gather(mine.astype(jnp.bfloat16), 'tm', tiled=True)  13.1 us
    unnamed x24, local copies, waits for them, and re-layouts  10.6 us
    dot_general x1, matrix products, on_device(): jnp.einsum('rn,cnh->crh', normed, pair, preferred_element_type=jnp.float32)  9.52 us
  transfers between devices with their start and end apart: 3, of which 2 were waited for; matrix products, arithmetic and copies ran while one was open for 18% of the time, Pallas kernels for 0%

commit v1 on v0

--- a/solution.py
+++ b/solution.py
@@ -9,7 +9,15 @@
 
 def gathered(weights):
     columns_full = lax.all_gather(jnp.stack(weights), "space", axis=2, tiled=True)
-    return lax.all_gather(columns_full, "tm", axis=1, tiled=True)
+    return jnp.concatenate(
+        lax.all_to_all(
+            jnp.stack([columns_full for _ in range(lax.axis_size("tm"))], 0),
+            axis_name="tm",
+            split_axis=0,
+            concat_axis=0,
+        ),
+        1,
+    )
 
 
 def on_device(latent_tokens, norm_gain, w_query, w_key, w_value, out_gain, block_ids):

time: 275 us -> 362 us (1.32)
  waiting for transfers between devices: 45.1 us -> 108 us
  starting transfers between devices: 0.09 us -> 21.1 us
  local copies, waits for them, and re-layouts: 29.9 us -> 36 us
    all_to_all x0 -> x2, waiting for transfers between devices: none -> 93.2 us  [gathered(): lax.all_to_all(jnp.stack([columns_full for _ in range(lax.axis_size('tm')...]
    all_gather x2 -> x0, waiting for transfers between devices: 32 us -> none  [gathered(): return lax.all_gather(columns_full, 'tm', axis=1, tiled=True)]
    all_to_all x0 -> x2, starting transfers between devices: none -> 21.1 us  [gathered(): lax.all_to_all(jnp.stack([columns_full for _ in range(lax.axis_size('tm')...]
    another operation x0 -> x3, local copies, waits for them, and re-layouts: none -> 17.5 us  [the longest x2 9.41 us: gathered(): jnp.stack([columns_full for _ in range(lax.axis_size('tm'))], 0)]
    unnamed x24 -> x25, local copies, waits for them, and re-layouts: 10.6 us -> 1.89 us
  transfers between devices with their start and end apart: 3 -> 3, of which waited for: 2 -> 2; matrix products, arithmetic and copies ran while one was open for 18% -> 12% of each run, Pallas kernels for 0% -> 0%
where the time goes in v1:
time: 362 us; the launch traced here: 361 us
  blocking collectives  157 us (43%)
  waiting for transfers between devices  108 us (30%)
  local copies, waits for them, and re-layouts  36 us (10%)
  starting transfers between devices  21.1 us (6%)
  matrix products  19.6 us (5%)
  between operations  14.9 us (4%)
  other arithmetic  4.68 us (1%)
    all_to_all x2, waiting for transfers between devices, gathered(): lax.all_to_all(jnp.stack([columns_full for _ in range(lax.axis_size('tm')...  93.2 us
    unnamed x2, blocking collectives  75.6 us
    all_gather x2, blocking collectives, gathered(): lax.all_gather(jnp.stack(weights), 'space', axis=2, tiled=True)  54.2 us
    all_gather x1, blocking collectives, on_device(): lax.all_gather(carried.astype(jnp.bfloat16), 'space', axis=1, tiled=True)  27 us
    all_to_all x2, starting transfers between devices, gathered(): lax.all_to_all(jnp.stack([columns_full for _ in range(lax.axis_size('tm')...  21.1 us
    all_gather x1, waiting for transfers between devices, on_device(): everyone = lax.all_gather(mine.astype(jnp.bfloat16), 'tm', tiled=True)  14.7 us
    another operation x2, local copies, waits for them, and re-layouts, gathered(): jnp.stack([columns_full for _ in range(lax.axis_size('tm'))], 0)  9.41 us
    dot_general x1, matrix products, on_device(): jnp.einsum('rn,cnh->crh', normed, pair, preferred_element_type=jnp.float32)  9.13 us
  transfers between devices with their start and end apart: 3, of which 2 were waited for; matrix products, arithmetic and copies ran while one was open for 12% of the time, Pallas kernels for 0%

profile of v1, /device:TPU:6, one launch (start us, length us, event | category | flops | bytes accessed | tf_op | source)
XLA Modules:
  0.0 361.0 jit_solution(17863082734008274876)
XLA Ops:
  6.5 0.8 pad_maximum_fusion
  7.5 29.2 %all_gather.18 = bf16[2,70,1120]{1,0,2:T(2,128)(2,1)S(1)} all-gather(bf16[2,70,140]{1,0,2:T(2,128)(2,1)S(1)} %copy.41), channel_id=1, replica_groups=mesh['tm'=32,'space'=8] {'space'}, dimensions={2}, use_global_device_ids=true | all-gather | bytes 352800 | tf_op jit(solution)/shard_map/all_gather | solution.py:11
  36.7 1.4 copy.42
  38.1 6.8 %stack.15 = bf16[32,2,70,1120]{3,1,2,0:T(2,128)(2,1)} broadcast(bf16[2,70,1120]{2,0,1:T(2,128)(2,1)S(1)} %copy.42), dimensions={1,2,3} | broadcast | bytes 10348800 | tf_op jit(solution)/shard_map/stack | solution.py:14
  44.9 7.8 %all-to-all-start = ((bf16[32,2,70,1120]{3,1,2,0:T(2,128)(2,1)}), bf16[32,2,70,1120]{3,1,2,0:T(2,128)(2,1)}, u32[]{:S(2)}, u32[]{:S(2)}) async-start(bf16[32,2,70,1120]{3,1,2,0:T(2,128)(2,1)} %stack.15), calls=%async_computation | async-start | bytes 20643840 | tf_op jit(solution)/shard_map/all_to_all | solution.py:13
  52.8 25.0 %all-gather.1 = bf16[8,140,70]{2,1,0:T(8,128)(2,1)S(1)} all-gather(bf16[1,140,70]{2,1,0:T(8,128)(2,1)S(1)} %bitcast.46), channel_id=2, replica_groups=mesh['tm'=32,'space'=8] {'space'}, dimensions={0}, use_global_device_ids=true | all-gather | bytes 176400 | tf_op jit(solution)/shard_map/all_gather | solution.py:11
  78.1 0.6 dynamic-slice.1
  79.3 0.5 fusion.2
  79.8 1.8 fusion.4
  81.7 93.2 %all-to-all-done = bf16[32,2,70,1120]{3,1,2,0:T(2,128)(2,1)} async-done(((bf16[32,2,70,1120]{3,1,2,0:T(2,128)(2,1)}), bf16[32,2,70,1120]{3,1,2,0:T(2,128)(2,1)}, u32[]{:S(2)}, u32[]{:S(2)}) %all-to-all-start) | async-done | bytes 10035232 | tf_op jit(solution)/shard_map/all_to_all | solution.py:13
  174.9 2.6 stack.17
  177.6 13.3 %all-to-all-start.1 = ((bf16[32,1,70,1120]{3,2,1,0:T(8,128)(2,1)}), bf16[32,1,70,1120]{3,2,1,0:T(8,128)(2,1)}, u32[]{:S(2)}, u32[]{:S(2)}) async-start(bf16[32,1,70,1120]{3,2,1,0:T(8,128)(2,1)} %stack.17), calls=%async_computation.1 | async-start | bytes 10616832 | tf_op jit(solution)/shard_map/all_to_all | solution.py:13
  190.9 9.1 %fusion.5 = bf16[2,448,1120]{2,1,0:T(8,128)(2,1)S(1)} fusion(bf16[448,2240,1]{1,0,2:T(8,128)(2,1)S(1)} %bitcast.43, bf16[2,2240,1120]{2,0,1:T(2,128)(2,1)} %bitcast.5), kind=kOutput, calls=%fused_computation.7 | convolution fusion | flops 4495769600 | bytes 14049280 | tf_op jit(solution)/shard_map/rn,cnh->crh/dot_general | solution.py:31
  200.1 1.2 fusion.15
  201.2 3.4 reshape.102
  204.7 3.1 reshape.103
  207.8 2.1 fusion.18
  209.9 4.2 %copy.48 = f32[2,1120,112]{2,0,1:T(2,128)S(1)} copy(f32[2,1120,112]{2,1,0:T(8,128)S(1)} %bitcast.41) | data formatting | bytes 2007040 | tf_op jit(solution)/shard_map/reshape | solution.py:37
  214.1 60.8 %all-reduce.3 = bf16[2,1120,112]{2,0,1:T(2,128)(2,1)S(1)} all-reduce(f32[2,1120,112]{2,0,1:T(2,128)S(1)} %copy.48), channel_id=3, replica_groups=mesh['tm'=32,'space'=8] {'space'}, use_global_device_ids=true, to_apply=%region_1.2.clone | all-reduce | flops 250880 | bytes 1505280
  274.9 0.6 copy.49
  275.7 0.6 dynamic-slice
  277.0 0.2 dynamic-update-slice
  277.2 14.8 %all-reduce = s32[64]{0:T(128)S(1)} all-reduce(s32[64]{0:T(128)S(1)} %dynamic-update-slice), channel_id=1, replica_groups=mesh['tm'=32,'space'=8] {'tm'}, use_global_device_ids=true, to_apply=%add | all-reduce | flops 64 | bytes 512
  292.0 8.1 %reshape.90 = bf16[2240,1120]{1,0:T(8,128)(2,1)} reshape(bf16[32,1,70,1120]{3,2,1,0:T(8,128)(2,1)} %all-to-all-done.1) | data formatting | bytes 10035200 | tf_op jit(solution)/shard_map/reshape.2
  300.2 5.3 %fusion.9 = bf16[1,448,1120]{2,1,0:T(8,128)(2,1)S(1)} fusion(bf16[448,2240]{1,0:T(8,128)(2,1)S(1)} %bitcast.44, bf16[2240,1120]{1,0:T(8,128)(2,1)} %reshape.90), kind=kOutput, calls=%fused_computation.10 | convolution fusion | flops 2248888320 | bytes 8028160 | tf_op jit(solution)/shard_map/rn,cnh->crh/dot_general | solution.py:45
  305.4 2.2 reshape.105
  307.6 14.7 %all-gather.4.cloned.1.call-done = bf16[64,140,112]{2,1,0:T(8,128)(2,1)} async-done(((bf16[2,140,112]{2,1,0:T(8,128)(2,1)}), bf16[64,140,112]{2,1,0:T(8,128)(2,1)}) %all-gather.4.cloned.1.call-update) | async-done | bytes 2007056 | tf_op jit(solution)/shard_map/all_gather | solution.py:39
  322.3 2.2 fusion.21
  324.5 27.0 %all_gather.20 = bf16[2,1120,112]{2,0,1:T(2,128)(2,1)S(1)} all-gather(bf16[2,140,112]{2,0,1:T(2,128)(2,1)S(1)} %fusion.21), channel_id=1, replica_groups=mesh['tm'=32,'space'=8] {'space'}, dimensions={1}, use_global_device_ids=true | all-gather | bytes 564480 | tf_op jit(solution)/shard_map/all_gather | solution.py:43
  351.5 0.9 fusion.10
  352.5 0.4 fusion.12
  352.8 1.4 copy.57
  (30 shorter events, 0.8 us)
Async XLA Ops:
  44.8 7.8 %copy-start.3 = (bf16[70,140]{1,0:T(8,128)(2,1)S(1)}, bf16[70,140]{1,0:T(8,128)(2,1)}, u32[]{:S(2)}) copy-start(bf16[70,140]{1,0:T(8,128)(2,1)} %param.9) | copy-start | bytes 58804
  44.9 33.2 %copy-start.8 = (u32[256]{0:T(256)S(1)}, u32[256]{0:T(256)}, u32[]{:S(2)}) copy-start(u32[256]{0:T(256)} %constant.27) | copy-start | bytes 3076
  44.9 34.5 %copy-start = (bf16[2,224,2240]{2,1,0:T(8,128)(2,1)S(1)}, bf16[2,224,2240]{2,1,0:T(8,128)(2,1)}, u32[]{:S(2)}) copy-start(bf16[2,224,2240]{2,1,0:T(8,128)(2,1)} %param.7) | copy-start | bytes 6021124
  44.9 130.1 %all-to-all-start = ((bf16[32,2,70,1120]{3,1,2,0:T(2,128)(2,1)}), bf16[32,2,70,1120]{3,1,2,0:T(2,128)(2,1)}, u32[]{:S(2)}, u32[]{:S(2)}) async-start(bf16[32,2,70,1120]{3,1,2,0:T(2,128)(2,1)} %stack.15), calls=%async_computation | async-start | bytes 20643840 | tf_op jit(solution)/shard_map/all_to_all | solution.py:13
  52.6 27.2 %copy-start.4 = (f32[2240]{0:T(1024)S(1)}, f32[2240]{0:T(1024)}, u32[]{:S(2)}) copy-start(f32[2240]{0:T(1024)} %param.8) | copy-start | bytes 26884
  177.6 13.4 %copy-start.1 = (bf16[2,224,2240]{2,1,0:T(8,128)(2,1)S(1)}, bf16[2,224,2240]{2,1,0:T(8,128)(2,1)}, u32[]{:S(2)}) copy-start(bf16[2,224,2240]{2,1,0:T(8,128)(2,1)} %fusion.4) | copy-start | bytes 6021124
  177.6 114.4 %all-to-all-start.1 = ((bf16[32,1,70,1120]{3,2,1,0:T(8,128)(2,1)}), bf16[32,1,70,1120]{3,2,1,0:T(8,128)(2,1)}, u32[]{:S(2)}, u32[]{:S(2)}) async-start(bf16[32,1,70,1120]{3,2,1,0:T(8,128)(2,1)} %stack.17), calls=%async_computation.1 | async-start | bytes 10616832 | tf_op jit(solution)/shard_map/all_to_all | solution.py:13
  190.9 131.5 %all-gather.4.cloned.1.call-start = ((), (), s32[]{:S(2)}) async-start(), calls=%async_computation.2 | async-start | bytes 2433024 | tf_op jit(solution)/shard_map/all_gather | solution.py:39
  209.9 65.7 %copy-start.5 = (f32[1120]{0:T(1024)S(1)}, f32[1120]{0:T(1024)}, u32[]{:S(2)}) copy-start(f32[1120]{0:T(1024)} %param.12) | copy-start | bytes 13444
  209.9 65.8 %copy-start.7 = (u32[256]{0:T(256)S(1)}, u32[256]{0:T(256)}, u32[]{:S(2)}) copy-start(u32[256]{0:T(256)} %constant.21) | copy-start | bytes 3076
  209.9 67.1 %copy-start.6 = (s32[2]{0:T(128)S(1)}, s32[2]{0:T(128)}, u32[]{:S(2)}) copy-start(s32[2]{0:T(128)} %param.13) | copy-start | bytes 28
  292.0 8.1 %copy-start.2 = (bf16[2,224,2240]{2,1,0:T(8,128)(2,1)S(1)}, bf16[2,224,2240]{2,1,0:T(8,128)(2,1)}, u32[]{:S(2)}) copy-start(bf16[2,224,2240]{2,1,0:T(8,128)(2,1)} %fusion.4) | copy-start | bytes 6021124
Sparse Core Ops, SparseCore 0:
  275.7 46.5 all-gather.3
